TPU v7x, 32 devices: a whole 2x2x4 slice. The times are simulated.
32 devices in a mesh: sample: 2 (over x), row: 16 (over z, y, core).
Axes of the slice: x: 2, y: 2, z: 4, core: 2. Of those that a mesh axis runs over, the one named last changes fastest.
Arguments:
- sample_index: int32 [2], P('sample'), parts along dimension 0, may hold values from 0 to 32767
- lattice_vector: int32 [1024], replicated, may hold values from 1 to 32767
- mode_table: int32 [2, 1024], replicated, may hold values from -16 to 31, as said below
- connectivity: int32 [3, 32768], replicated, may hold values from 0 to 16639, as said below
- density: bfloat16 [64, 32768], P(None, 'row'), may hold values from -3.5 to 3.5
Outputs:
- potential: float32 [8192, 64], P(('sample', 'row')), parts along dimension 0
There are 2 independent parts, one for each index of `sample`. A program takes and returns all parts, laid end to end along the dimension named above; an argument that names none is the same for every part. Nothing has to cross between parts.
Inputs may be any that keep to these rules, and one draw needn't show every extreme that they name: `mode_table`: the 1024 columns are distinct frequency pairs, the polar one from 0 to 31 and the azimuthal one from -16 to 15. `connectivity`: vertex i * 256 + j lies on latitude cycle i and azimuth j. The columns are the triangles of that grid, two per cell between neighbouring cycles (azimuth wrapping around), each once and oriented with outward normals, in random order.
All inputs are finite; a program needn't handle non-finite values.
Results may differ from a plain program's by a relative error of at most 0.0035.
Values may be sent and summed in bfloat16 or wider, within the bound.
A program may use at most 256 MiB of HBM per device.

v0:
```python
import math

import jax
import jax.numpy as jnp
from jax import lax
from jax.sharding import PartitionSpec as P

NLAT = 32768
NPH = 256
BAND_DEV = 256


def vertex_grid(sample_index, lattice_vector, mode_table, cycle_count):
    lattice_steps = sample_index[0] * lattice_vector % NLAT
    shifts = lattice_steps.astype(jnp.float32) / NLAT - 0.5
    polar_freq = mode_table[0].astype(jnp.float32)
    azim_freq = mode_table[1].astype(jnp.float32)
    mode_coef = 0.8 * shifts / (1.0 + polar_freq + jnp.abs(azim_freq)) ** 2
    polar_angle = math.pi * (jnp.arange(cycle_count, dtype=jnp.float32) + 1.0) / (cycle_count + 1)
    azimuth = 2.0 * math.pi * jnp.arange(NPH, dtype=jnp.float32) / NPH
    polar_phase = polar_angle[:, None] * polar_freq[None, :]
    azim_phase = azim_freq[:, None] * azimuth[None, :]
    cos_part = jnp.dot(
        jnp.cos(polar_phase) * mode_coef[None, :],
        jnp.cos(azim_phase),
        precision=lax.Precision.HIGHEST,
    )
    sin_part = jnp.dot(
        jnp.sin(polar_phase) * mode_coef[None, :],
        jnp.sin(azim_phase),
        precision=lax.Precision.HIGHEST,
    )
    radius = jnp.exp(cos_part - sin_part)
    cycle_sin = jnp.sin(polar_angle)[:, None]
    coord_x = radius * cycle_sin * jnp.cos(azimuth)[None, :]
    coord_y = radius * cycle_sin * jnp.sin(azimuth)[None, :]
    coord_z = radius * jnp.cos(polar_angle)[:, None]
    return jnp.stack([coord_x, coord_y, coord_z]).reshape(3, cycle_count * NPH)


def panel_geometry(vertices, corners):
    corner_one = vertices[:, corners[0]]
    corner_two = vertices[:, corners[1]]
    corner_three = vertices[:, corners[2]]
    centers = (corner_one + corner_two + corner_three) / 3.0
    edge_one = corner_two - corner_one
    edge_two = corner_three - corner_one
    area_vectors = 0.5 * jnp.stack(
        [
            edge_one[1] * edge_two[2] - edge_one[2] * edge_two[1],
            edge_one[2] * edge_two[0] - edge_one[0] * edge_two[2],
            edge_one[0] * edge_two[1] - edge_one[1] * edge_two[0],
        ]
    )
    return (centers, area_vectors)


def kernel_tile(target_centers, target_ids, source_centers, source_areas, source_ids):
    delta_x = target_centers[0][:, None] - source_centers[0][None, :]
    delta_y = target_centers[1][:, None] - source_centers[1][None, :]
    delta_z = target_centers[2][:, None] - source_centers[2][None, :]
    dist_sq = delta_x * delta_x + delta_y * delta_y + delta_z * delta_z
    self_pair = target_ids[:, None] == source_ids[None, :]
    safe_dist = jnp.where(self_pair, 1.0, dist_sq)
    numerator = (
        delta_x * source_areas[0][None, :]
        + delta_y * source_areas[1][None, :]
        + delta_z * source_areas[2][None, :]
    )
    kernel_value = numerator / (4.0 * math.pi * safe_dist * jnp.sqrt(safe_dist))
    return jnp.where(self_pair, 0.0, kernel_value).astype(jnp.bfloat16)


def apply_tile(tile, density_block):
    return lax.dot_general(
        tile, density_block, (((1,), (1,)), ((), ())), preferred_element_type=jnp.float32
    )


def per_device(sample_index, lattice_vector, mode_table, connectivity, density):
    columns, src_dev = density.shape
    band_dev = BAND_DEV
    row_total = lax.axis_size("row")
    row_index = lax.axis_index("row")
    panel_total = src_dev * row_total
    cycle_count = panel_total // (2 * NPH) + 1
    vertices = vertex_grid(sample_index, lattice_vector, mode_table, cycle_count)
    own_first = row_index * src_dev
    own_ids = own_first + jnp.arange(src_dev, dtype=jnp.int32)
    own_corners = lax.dynamic_slice_in_dim(connectivity, own_first, src_dev, 1)
    own_centers, own_areas = panel_geometry(vertices, own_corners)
    local_term = 0.5 * density[:, :band_dev].astype(jnp.float32).T
    band_centers = lax.all_gather(own_centers[:, :band_dev], "row", axis=1, tiled=True)
    block = math.gcd(band_dev * lax.axis_size("row"), 1024)

    def one_block(turn):
        first_row = turn * block
        rows = first_row + jnp.arange(block, dtype=jnp.int32)
        target_ids = rows // band_dev * src_dev + rows % band_dev
        target_centers = lax.dynamic_slice_in_dim(band_centers, first_row, block, 1)
        tile = kernel_tile(target_centers, target_ids, own_centers, own_areas, own_ids)
        return apply_tile(tile, density)

    blocks = lax.map(
        one_block, jnp.arange(band_dev * lax.axis_size("row") // block, dtype=jnp.int32)
    )
    sums = lax.psum_scatter(
        blocks.reshape(band_dev * lax.axis_size("row"), columns),
        "row",
        scatter_dimension=0,
        tiled=True,
    )
    return local_term + sums


def solution(mesh):
    placed = (P("sample"), P(), P(), P(), P(None, "row"))
    return jax.shard_map(
        per_device,
        mesh=mesh,
        in_specs=placed,
        out_specs=P(("sample", "row"), None),
        check_vma=False,
    )
```

profile of v0, /device:TPU:0, one launch (start us, length us, event | category | flops | bytes accessed | tf_op | source)
XLA Modules:
  0.0 187.7 jit_solution(3020884002444759545)
XLA Ops:
  6.5 0.8 slice_convert_fusion.1
  7.3 0.7 broadcast_add_fusion
  8.8 0.7 fusion.46
  9.5 5.1 %fusion.25 = f32[65,256]{1,0:T(8,128)S(1)} fusion(f32[256]{0:T(256)S(1)} %iota_multiply_fusion, f32[1024]{0:T(1024)S(1)} %bitcast.108, f32[1024]{0:T(1024)S(1)} %fusion.46, f32[1024]{0:T(1024)S(1)} %bitcast.110, f32[65]{0:T(128)S(1)} %add_multiply_fusion), kind=kOutput, calls=%fused_computation.44 | convolution fusion | flops 204867584 | bytes 80132 | tf_op jit(solution)/shard_map/dot_general | solution.py:23
  14.6 5.2 %multiply_bitcast_fusion.2 = (f32[1,1,65,256]{3,2,1,0:T(8,128)S(1)}, f32[1,1,65,256]{3,2,1,0:T(8,128)S(1)}, f32[1,1,65,256]{3,2,1,0:T(8,128)S(1)}) fusion(f32[256]{0:T(256)S(1)} %get-tuple-element.196, f32[65]{0:T(128)S(1)} %get-tuple-element.198, f32[256]{0:T(256)S(1)} %get-tuple-element.195, f32[65]{0:T(128)S(1)} %get-tuple-element.197, ...), kind=kOutput, calls=%fused_computation.62 | convolution fusion | flops 204950784 | bytes 282380 | tf_op jit(solution)/shard_map/dot_general | solution.py:28
  20.3 5.3 %copy.38 = f32[3,16640]{0,1:T(8,128)} copy(f32[3,16640]{1,0:T(4,128)S(1)} %pad_maximum_fusion) | data formatting | bytes 399360 | tf_op jit(solution)/shard_map/stack | solution.py:38
  25.6 1.0 compare_select_fusion.4
  26.6 8.9 %gather_fusion = f32[2048,3]{1,0:T(8,128)S(1)} fusion(f32[3,16640]{0,1:T(8,128)} %copy.38, s32[2048]{0:T(1024)S(1)} %broadcast_clamp_fusion.2), kind=kCustom, calls=%fused_computation | custom fusion | bytes 57344 | tf_op jit(solution)/shard_map/gather | solution.py:42
  35.8 8.9 %gather_fusion.1 = f32[2048,3]{1,0:T(8,128)S(1)} fusion(f32[3,16640]{0,1:T(8,128)} %copy.38, s32[2048]{0:T(1024)S(1)} %broadcast_clamp_fusion.1), kind=kCustom, calls=%fused_computation.1 | custom fusion | bytes 57344 | tf_op jit(solution)/shard_map/gather | solution.py:43
  45.0 8.9 %gather_fusion.2 = f32[2048,3]{1,0:T(8,128)S(1)} fusion(f32[3,16640]{0,1:T(8,128)} %copy.38, s32[2048]{0:T(1024)S(1)} %broadcast_clamp_fusion), kind=kCustom, calls=%fused_computation.2 | custom fusion | bytes 57344 | tf_op jit(solution)/shard_map/gather | solution.py:44
  54.3 23.3 %all_gather.3 = f32[3,4096]{1,0:T(4,128)S(1)} all-gather(f32[3,256]{1,0:T(4,128)S(1)} %slice.127), channel_id=1, replica_groups=mesh['sample'=2,'row'=16] {'row'}, dimensions={1}, use_global_device_ids=true | all-gather | bytes 52224 | tf_op jit(solution)/shard_map/all_gather | solution.py:93
  77.7 45.2 %while.13 = (s32[]{:T(128)}, f32[4,1024,64]{1,0,2:T(4,128)S(1)}, s32[4]{0:T(128)S(1)}, f32[3,4096]{1,0:T(4,128)S(1)}, f32[3,2048]{1,0:T(4,128)S(1)}, /*index=5*/...) while((s32[]{:T(128)}, f32[4,1024,64]{1,0,2:T(4,128)S(1)}, ...), condition=%wide.region_1.2_spmd.clone, body=%wide.region_0.1_spmd.clone.sunk | while | flops 310403072 | bytes 1781999 | solution.py:104
  77.7 0.7 dynamic_slice.20
  79.1 7.5 %fusion.65 = f32[1,1024,64]{1,2,0:T(8,128)S(1)} fusion(bf16[64,2048]{1,0:T(8,128)(2,1)S(1)} %get-tuple-element.300, f32[2048]{0:T(1024)S(1)} %bitcast.98, f32[2048]{0:T(1024)S(1)} %bitcast.95, f32[1024]{0:T(1024)S(1)} %bitcast.102, f32[2048]{0:T(1024)S(1)} %bitcast.97, f32[2048]{0:T(1024)S(1)} %bitcast.96, f32[1024]{0:T(1024)S(1)} %bitcast.101, ...), kind=kOutput, calls=%fused_computation.20.clone.1 | convolution fusion | flops 310378496 | bytes 598016 | tf_op jit(solution)/shard_map/while/body/eval_jaxpr/dot_general | solution.py:75
  86.9 2.1 %dynamic_update_slice.9 = f32[4,1024,64]{1,0,2:T(4,128)S(1)} dynamic-update-slice(f32[4,1024,64]{1,0,2:T(4,128)S(1)} %get-tuple-element.281, f32[1,1024,64]{1,0,2:T(1,128)S(1)} %copy.52, s32[]{:T(128)} %get-tuple-element.280, s32[]{:T(128)} %constant.123.clone.1..sunk, s32[]{:T(128)} %constant.123.clone.1..sunk) | dynamic-update-slice | bytes 524292 | tf_op jit(solution)/shard_map/while/body/jit(dynamic_update_index_in_dim)/dynamic_update_slice | solution.py:104
  90.4 7.5 %fusion.65 = f32[1,1024,64]{1,2,0:T(8,128)S(1)} fusion(bf16[64,2048]{1,0:T(8,128)(2,1)S(1)} %get-tuple-element.300, f32[2048]{0:T(1024)S(1)} %bitcast.98, f32[2048]{0:T(1024)S(1)} %bitcast.95, f32[1024]{0:T(1024)S(1)} %bitcast.102, f32[2048]{0:T(1024)S(1)} %bitcast.97, f32[2048]{0:T(1024)S(1)} %bitcast.96, f32[1024]{0:T(1024)S(1)} %bitcast.101, ...), kind=kOutput, calls=%fused_computation.20.clone.1 | convolution fusion | flops 310378496 | bytes 598016 | tf_op jit(solution)/shard_map/while/body/eval_jaxpr/dot_general | solution.py:75
  98.2 2.1 %dynamic_update_slice.9 = f32[4,1024,64]{1,0,2:T(4,128)S(1)} dynamic-update-slice(f32[4,1024,64]{1,0,2:T(4,128)S(1)} %get-tuple-element.281, f32[1,1024,64]{1,0,2:T(1,128)S(1)} %copy.52, s32[]{:T(128)} %get-tuple-element.280, s32[]{:T(128)} %constant.123.clone.1..sunk, s32[]{:T(128)} %constant.123.clone.1..sunk) | dynamic-update-slice | bytes 524292 | tf_op jit(solution)/shard_map/while/body/jit(dynamic_update_index_in_dim)/dynamic_update_slice | solution.py:104
  101.7 7.5 %fusion.65 = f32[1,1024,64]{1,2,0:T(8,128)S(1)} fusion(bf16[64,2048]{1,0:T(8,128)(2,1)S(1)} %get-tuple-element.300, f32[2048]{0:T(1024)S(1)} %bitcast.98, f32[2048]{0:T(1024)S(1)} %bitcast.95, f32[1024]{0:T(1024)S(1)} %bitcast.102, f32[2048]{0:T(1024)S(1)} %bitcast.97, f32[2048]{0:T(1024)S(1)} %bitcast.96, f32[1024]{0:T(1024)S(1)} %bitcast.101, ...), kind=kOutput, calls=%fused_computation.20.clone.1 | convolution fusion | flops 310378496 | bytes 598016 | tf_op jit(solution)/shard_map/while/body/eval_jaxpr/dot_general | solution.py:75
  109.4 2.1 %dynamic_update_slice.9 = f32[4,1024,64]{1,0,2:T(4,128)S(1)} dynamic-update-slice(f32[4,1024,64]{1,0,2:T(4,128)S(1)} %get-tuple-element.281, f32[1,1024,64]{1,0,2:T(1,128)S(1)} %copy.52, s32[]{:T(128)} %get-tuple-element.280, s32[]{:T(128)} %constant.123.clone.1..sunk, s32[]{:T(128)} %constant.123.clone.1..sunk) | dynamic-update-slice | bytes 524292 | tf_op jit(solution)/shard_map/while/body/jit(dynamic_update_index_in_dim)/dynamic_update_slice | solution.py:104
  113.0 7.5 %fusion.65 = f32[1,1024,64]{1,2,0:T(8,128)S(1)} fusion(bf16[64,2048]{1,0:T(8,128)(2,1)S(1)} %get-tuple-element.300, f32[2048]{0:T(1024)S(1)} %bitcast.98, f32[2048]{0:T(1024)S(1)} %bitcast.95, f32[1024]{0:T(1024)S(1)} %bitcast.102, f32[2048]{0:T(1024)S(1)} %bitcast.97, f32[2048]{0:T(1024)S(1)} %bitcast.96, f32[1024]{0:T(1024)S(1)} %bitcast.101, ...), kind=kOutput, calls=%fused_computation.20.clone.1 | convolution fusion | flops 310378496 | bytes 598016 | tf_op jit(solution)/shard_map/while/body/eval_jaxpr/dot_general | solution.py:75
  120.7 2.1 %dynamic_update_slice.9 = f32[4,1024,64]{1,0,2:T(4,128)S(1)} dynamic-update-slice(f32[4,1024,64]{1,0,2:T(4,128)S(1)} %get-tuple-element.281, f32[1,1024,64]{1,0,2:T(1,128)S(1)} %copy.52, s32[]{:T(128)} %get-tuple-element.280, s32[]{:T(128)} %constant.123.clone.1..sunk, s32[]{:T(128)} %constant.123.clone.1..sunk) | dynamic-update-slice | bytes 524292 | tf_op jit(solution)/shard_map/while/body/jit(dynamic_update_index_in_dim)/dynamic_update_slice | solution.py:104
  122.8 1.6 copy.50
  124.4 54.9 %reduce-scatter.2.cloned.1.call-done = f32[256,64]{0,1:T(8,128)} async-done(((f32[4096,64]{0,1:T(8,128)}), f32[256,64]{0,1:T(8,128)}) %reduce-scatter.2.cloned.1.call-update) | async-done | bytes 65552 | tf_op jit(solution)/shard_map/reduce_scatter | solution.py:107
  179.3 1.5 bitcast_add_fusion
  (47 shorter events, 5.2 us)
Async XLA Ops:
  6.5 71.1 %copy-start = (bf16[64,2048]{1,0:T(8,128)(2,1)S(1)}, bf16[64,2048]{1,0:T(8,128)(2,1)}, u32[]{:S(2)}) copy-start(bf16[64,2048]{1,0:T(8,128)(2,1)} %param.11) | copy-start | bytes 786436
  6.5 172.8 %reduce-scatter.2.cloned.1.call-start = ((), (), s32[]{:S(2)}) async-start(), calls=%async_computation.1 | async-start | bytes 1114112 | tf_op jit(solution)/shard_map/reduce_scatter | solution.py:107
Sparse Core Ops, SparseCore 0:
  124.6 54.7 reduce-scatter.1
where the time goes:
time: 188 us
  waiting for transfers between devices  54.9 us (29%)
  local copies, waits for them, and re-layouts  47.3 us (25%)
  matrix products  40.1 us (21%)
  blocking collectives  23.3 us (12%)
  between operations  14.2 us (8%)
  other arithmetic  5.11 us (3%)
  loops' own time  2.73 us (1%)
    reduce_scatter x1, waiting for transfers between devices, per_device(): lax.psum_scatter(blocks.reshape(band_dev * lax.axis_size('row'), columns)...  54.9 us
    dot_general x4, matrix products, apply_tile(): lax.dot_general(tile, density_block, (((1,), (1,)), ((), ())), preferred_...  29.8 us
    all_gather x1, blocking collectives, per_device(): lax.all_gather(own_centers[:, :band_dev], 'row', axis=1, tiled=True)  23.3 us
    dynamic_update_slice x8, local copies, waits for them, and re-layouts, per_device(): lax.map(one_block, jnp.arange(band_dev * lax.axis_size('row') // block, d...  9.44 us
    gather x2, local copies, waits for them, and re-layouts, panel_geometry(): corner_three = vertices[:, corners[2]]  9.22 us
    gather x2, local copies, waits for them, and re-layouts, panel_geometry(): corner_two = vertices[:, corners[1]]  9.22 us
    gather x2, local copies, waits for them, and re-layouts, panel_geometry(): corner_one = vertices[:, corners[0]]  9.21 us
    another operation x1, local copies, waits for them, and re-layouts, vertex_grid(): return jnp.stack([coord_x, coord_y, coord_z]).reshape(3, cycle_count * NPH)  5.32 us
  transfers between devices with their start and end apart: 1, of which 1 were waited for; matrix products, arithmetic and copies ran while one was open for 0% of the time, Pallas kernels for 0%

commit v1 on v0

v1 whole, which is shorter than its diff:
```python
import functools
import math

import jax
import jax.numpy as jnp
import numpy as np
from jax import lax
from jax.experimental import pallas as pl
from jax.experimental.pallas import tpu as pltpu
from jax.sharding import PartitionSpec as P

NLAT = 32768
NPH = 256
BAND_DEV = 256
POLAR = 32
AZIM = 32
AZIM_LOW = -16
KDIM = 32
CHUNK = 256
SRC_TILE = 256

F32 = jnp.float32
BF16 = jnp.bfloat16


def round_up(value, step):
    return -(-value // step) * step


def split3(value):
    high = value.astype(BF16)
    rest = value - high.astype(F32)
    mid = rest.astype(BF16)
    low = (rest - mid.astype(F32)).astype(BF16)
    return high, mid, low


def split3_np(value):
    import ml_dtypes

    value = value.astype(np.float32)
    high = value.astype(ml_dtypes.bfloat16)
    rest = value - high.astype(np.float32)
    mid = rest.astype(ml_dtypes.bfloat16)
    low = (rest - mid.astype(np.float32)).astype(ml_dtypes.bfloat16)
    return [high, mid, low]


def tables(cycle_count, padded):
    angle = np.pi * (np.arange(cycle_count) + 1.0) / (cycle_count + 1)
    azimuth = 2.0 * np.pi * np.arange(NPH) / NPH
    polar = np.arange(POLAR)
    azim = np.arange(AZIM) + AZIM_LOW
    pol = np.zeros((padded, 2 * POLAR), np.float32)
    pol[:cycle_count, :POLAR] = np.cos(angle[:, None] * polar[None])
    pol[:cycle_count, POLAR:] = np.sin(angle[:, None] * polar[None])
    azi = np.concatenate(
        [np.cos(azim[:, None] * azimuth[None]), -np.sin(azim[:, None] * azimuth[None])]
    ).astype(np.float32)
    after = np.roll(azimuth, -1)
    rows = []
    for field in (np.cos(azimuth), np.sin(azimuth), np.cos(after), np.sin(after)):
        rows += split3_np(field)
    azim_rows = np.zeros((16, NPH), rows[0].dtype)
    azim_rows[:12] = np.stack(rows)
    rows = []
    full = np.zeros(padded + 1)
    for func in (np.sin, np.cos):
        full[:cycle_count] = func(angle)
        rows += split3_np(full[:-1])
    for func in (np.sin, np.cos):
        full[:cycle_count] = func(angle)
        rows += split3_np(full[1:])
    polar_rows = np.zeros((16, padded), rows[0].dtype)
    polar_rows[:12] = np.stack(rows)
    return pol, azi, azim_rows, polar_rows


def dot_hi(left, right):
    return jnp.dot(left, right, precision=lax.Precision.HIGHEST, preferred_element_type=F32)


def geometry_kernel(
    padded, src_dev, row_total,
    sample_ref, lattice_ref, mode_ref, conn_ref, pol_ref, azi_ref, azim_rows_ref, polar_rows_ref,
    target_k_ref, target_c_ref, source_k_ref, source_b_ref,
    table_ref, rows_ref,
):
    steps = (sample_ref[0] * lattice_ref[...]) & (NLAT - 1)
    shifts = steps.astype(F32) / NLAT - 0.5
    polar = mode_ref[0:1, :]
    azim = mode_ref[1:2, :]
    scale = 1.0 + polar.astype(F32) + jnp.abs(azim.astype(F32))
    coef = 0.8 * shifts / (scale * scale)
    modes = coef.shape[1]
    at_polar = lax.broadcasted_iota(jnp.int32, (POLAR, modes), 0) == polar
    at_azim = lax.broadcasted_iota(jnp.int32, (AZIM, modes), 0) + AZIM_LOW == azim
    azim_hot = jnp.where(at_azim, 1.0, 0.0).astype(BF16)
    grid = jnp.zeros((POLAR, AZIM), F32)
    for part in split3(jnp.where(at_polar, coef, 0.0)):
        grid += lax.dot_general(part, azim_hot, (((1,), (1,)), ((), ())), preferred_element_type=F32)
    cos_half = dot_hi(grid, azi_ref[0:AZIM, :])
    sin_half = dot_hi(grid, azi_ref[AZIM:2 * AZIM, :])
    log_radius = dot_hi(pol_ref[:, 0:POLAR], cos_half) + dot_hi(pol_ref[:, POLAR:2 * POLAR], sin_half)
    radius = jnp.exp(log_radius)
    after = pltpu.roll(radius, NPH - 1, 1)
    for index, part in enumerate(split3(radius) + split3(after)):
        table_ref[index * padded:(index + 1) * padded, :] = part
    table_ref[6 * padded:6 * padded + 16, :] = azim_rows_ref[...]
    rows_ref[...] = jnp.zeros_like(rows_ref)

    def corners_of(corner):
        azim_all = corner & (NPH - 1)
        cycle_all = corner // NPH
        azim_k = [azim_all[k:k + 1, :] for k in range(3)]
        cycle_k = [cycle_all[k:k + 1, :] for k in range(3)]
        cycle0 = jnp.minimum(jnp.minimum(cycle_k[0], cycle_k[1]), cycle_k[2])
        low = jnp.minimum(jnp.minimum(azim_k[0], azim_k[1]), azim_k[2])
        high = jnp.maximum(jnp.maximum(azim_k[0], azim_k[1]), azim_k[2])
        azim0 = jnp.where(high - low > 1, high, low)
        hot = jnp.where(
            lax.broadcasted_iota(jnp.int32, (NPH, CHUNK), 0) == azim0, 1.0, 0.0
        ).astype(BF16)
        picked = jnp.dot(table_ref[...], hot, preferred_element_type=F32)
        near = picked[0:padded] + picked[padded:2 * padded] + picked[2 * padded:3 * padded]
        far = picked[3 * padded:4 * padded] + picked[4 * padded:5 * padded] + picked[5 * padded:6 * padded]
        tail = picked[6 * padded:6 * padded + 16]
        cycles = lax.broadcasted_iota(jnp.int32, (padded, CHUNK), 0)
        here = cycles == cycle0
        below = cycles == cycle0 + 1

        def take(mask, field):
            return jnp.sum(jnp.where(mask, field, 0.0), axis=0, keepdims=True)

        radius_of = ((take(here, near), take(here, far)), (take(below, near), take(below, far)))
        cycle_hot = jnp.where(here, 1.0, 0.0).astype(BF16)
        turn = jnp.dot(polar_rows_ref[...], cycle_hot, preferred_element_type=F32)

        def join(rows, start):
            return rows[start:start + 1] + rows[start + 1:start + 2] + rows[start + 2:start + 3]

        sin_t = (join(turn, 0), join(turn, 6))
        cos_t = (join(turn, 3), join(turn, 9))
        cos_f = (join(tail, 0), join(tail, 6))
        sin_f = (join(tail, 3), join(tail, 9))
        points = []
        for k in range(3):
            down = cycle_k[k] != cycle0
            side = azim_k[k] != azim0
            radius_k = jnp.where(
                down,
                jnp.where(side, radius_of[1][1], radius_of[1][0]),
                jnp.where(side, radius_of[0][1], radius_of[0][0]),
            )
            ring = radius_k * jnp.where(down, sin_t[1], sin_t[0])
            points.append((
                ring * jnp.where(side, cos_f[1], cos_f[0]),
                ring * jnp.where(side, sin_f[1], sin_f[0]),
                radius_k * jnp.where(down, cos_t[1], cos_t[0]),
            ))
        return points

    def center_of(points):
        return [(points[0][axis] + points[1][axis] + points[2][axis]) / 3.0 for axis in range(3)]

    def target_chunk(turn, carry):
        first = pl.multiple_of(turn * src_dev, src_dev)
        center = center_of(corners_of(conn_ref[:, pl.ds(first, CHUNK)]))
        place = pl.ds(pl.multiple_of(turn * CHUNK, CHUNK), CHUNK)
        for axis in range(3):
            target_c_ref[axis:axis + 1, place] = center[axis]
            high, mid, low = [part.astype(F32) for part in split3(center[axis])]
            for index, part in enumerate((high, high, high, mid, mid, low)):
                rows_ref[6 * axis + index:6 * axis + index + 1, :] = part
        rows_ref[18:21, :] = jnp.ones((3, CHUNK), F32)
        target_k_ref[:, place] = rows_ref[0:KDIM, :].astype(BF16)
        return carry

    def source_chunk(turn, carry):
        first = pl.multiple_of(lax.axis_index("row") * src_dev + turn * CHUNK, CHUNK)
        points = corners_of(conn_ref[:, pl.ds(first, CHUNK)])
        center = center_of(points)
        one = [points[1][axis] - points[0][axis] for axis in range(3)]
        two = [points[2][axis] - points[0][axis] for axis in range(3)]
        factor = 0.5 / (4.0 * math.pi)
        area = [
            factor * (one[1] * two[2] - one[2] * two[1]),
            factor * (one[2] * two[0] - one[0] * two[2]),
            factor * (one[0] * two[1] - one[1] * two[0]),
        ]
        for axis in range(3):
            high, mid, low = [part.astype(F32) for part in split3(area[axis])]
            for index, part in enumerate((high, mid, low, high, mid, high)):
                rows_ref[6 * axis + index:6 * axis + index + 1, :] = part
        base = -(center[0] * area[0] + center[1] * area[1] + center[2] * area[2])
        for index, part in enumerate(split3(base)):
            rows_ref[18 + index:19 + index, :] = part.astype(F32)
        for axis in range(3):
            rows_ref[KDIM + axis:KDIM + axis + 1, :] = center[axis]
        turned = rows_ref[...].T
        place = pl.ds(pl.multiple_of(turn * CHUNK, CHUNK), CHUNK)
        source_k_ref[place, :] = turned[:, 0:KDIM].astype(BF16)
        for axis in range(3):
            source_b_ref[axis, place, :] = jnp.broadcast_to(
                turned[:, KDIM + axis:KDIM + axis + 1], (CHUNK, 128)
            )
        return carry

    lax.fori_loop(0, row_total, target_chunk, 0)
    lax.fori_loop(0, src_dev // CHUNK, source_chunk, 0)


def pair_kernel(
    src_dev, row_total,
    target_k_ref, target_c_ref, source_k_ref, source_b_ref, density_ref,
    out_ref, send_buf, recv_buf, send_sem, recv_sem,
):
    me = lax.axis_index("row")
    peers = row_total - 1

    barrier = pltpu.get_barrier_semaphore()

    def greet(turn, carry):
        other = lax.rem(me + 1 + turn, row_total)
        pl.semaphore_signal(
            barrier, inc=1, device_id={"row": other}, device_id_type=pl.DeviceIdType.MESH
        )
        return carry

    lax.fori_loop(0, peers, greet, 0)

    def block(owner, own):
        place = pl.ds(pl.multiple_of(owner * BAND_DEV, BAND_DEV), BAND_DEV)
        target_k = target_k_ref[:, place]
        target = [target_c_ref[axis:axis + 1, place] for axis in range(3)]
        total = jnp.zeros((density_ref.shape[0], BAND_DEV), F32)
        for first in range(0, src_dev, SRC_TILE):
            part = slice(first, first + SRC_TILE)
            top = jnp.dot(source_k_ref[part, :], target_k, preferred_element_type=F32)
            dist = None
            for axis in range(3):
                wide = source_b_ref[axis, part, :]
                diff = target[axis] - jnp.concatenate([wide] * (BAND_DEV // 128), axis=1)
                dist = diff * diff if dist is None else dist + diff * diff
            if own and first < BAND_DEV:
                same = (
                    lax.broadcasted_iota(jnp.int32, dist.shape, 0) + first
                    == lax.broadcasted_iota(jnp.int32, dist.shape, 1)
                )
                inverse = lax.rsqrt(jnp.where(same, 1.0, dist))
                tile = jnp.where(same, 0.0, top * inverse * (inverse * inverse))
            else:
                inverse = lax.rsqrt(dist)
                tile = top * inverse * (inverse * inverse)
            total += jnp.dot(density_ref[:, part], tile.astype(BF16), preferred_element_type=F32)
        return total

    def copy(turn):
        return pltpu.make_async_remote_copy(
            src_ref=send_buf.at[turn],
            dst_ref=recv_buf.at[turn],
            send_sem=send_sem.at[turn],
            recv_sem=recv_sem.at[turn],
            device_id={"row": lax.rem(me + 1 + turn, row_total)},
            device_id_type=pl.DeviceIdType.MESH,
        )

    send_buf[0] = block(lax.rem(me + 1, row_total), False).astype(BF16)
    pl.semaphore_wait(barrier, peers)
    copy(0).start()

    def step(turn, carry):
        send_buf[turn] = block(lax.rem(me + 1 + turn, row_total), False).astype(BF16)
        copy(turn).start()
        return carry

    lax.fori_loop(1, peers, step, 0)
    out_ref[...] = block(me, True) + 0.5 * density_ref[:, 0:BAND_DEV].astype(F32)

    def collect(turn, carry):
        copy(turn).wait_recv()
        out_ref[...] += recv_buf[turn].astype(F32)
        return carry

    lax.fori_loop(0, peers, collect, 0)

    def finish(turn, carry):
        copy(turn).wait_send()
        return carry

    lax.fori_loop(0, peers, finish, 0)


def per_device(sample_index, lattice_vector, mode_table, connectivity, density):
    columns, src_dev = density.shape
    row_total = lax.axis_size("row")
    panel_total = src_dev * row_total
    cycle_count = panel_total // (2 * NPH) + 1
    padded = round_up(cycle_count, 16)
    band = BAND_DEV * row_total
    pol, azi, azim_rows, polar_rows = [jnp.asarray(t) for t in tables(cycle_count, padded)]
    vmem = pl.BlockSpec(memory_space=pltpu.VMEM)
    smem = pl.BlockSpec(memory_space=pltpu.SMEM)
    target_k, target_c, source_k, source_b = pl.pallas_call(
        functools.partial(geometry_kernel, padded, src_dev, row_total),
        out_shape=[
            jax.ShapeDtypeStruct((KDIM, band), BF16),
            jax.ShapeDtypeStruct((3, band), F32),
            jax.ShapeDtypeStruct((src_dev, KDIM), BF16),
            jax.ShapeDtypeStruct((3, src_dev, 128), F32),
        ],
        in_specs=[smem] + [vmem] * 7,
        out_specs=[vmem] * 4,
        scratch_shapes=[
            pltpu.VMEM((6 * padded + 16, NPH), BF16),
            pltpu.VMEM((KDIM + 8, CHUNK), F32),
        ],
        compiler_params=pltpu.CompilerParams(vmem_limit_bytes=40 << 20),
        name="geometry",
    )(
        sample_index, lattice_vector.reshape(1, -1), mode_table, connectivity,
        pol, azi, azim_rows, polar_rows,
    )
    sums = pl.pallas_call(
        functools.partial(pair_kernel, src_dev, row_total),
        out_shape=jax.ShapeDtypeStruct((columns, BAND_DEV), F32),
        in_specs=[vmem] * 5,
        out_specs=vmem,
        scratch_shapes=[
            pltpu.VMEM((row_total - 1, columns, BAND_DEV), BF16),
            pltpu.VMEM((row_total - 1, columns, BAND_DEV), BF16),
            pltpu.SemaphoreType.DMA((row_total - 1,)),
            pltpu.SemaphoreType.DMA((row_total - 1,)),
        ],
        compiler_params=pltpu.CompilerParams(
            collective_id=0, has_side_effects=True, vmem_limit_bytes=40 << 20
        ),
        name="pairs",
    )(target_k, target_c, source_k, source_b, density)
    return sums.T


def solution(mesh):
    placed = (P("sample"), P(), P(), P(), P(None, "row"))
    return jax.shard_map(
        per_device,
        mesh=mesh,
        in_specs=placed,
        out_specs=P(("sample", "row"), None),
        check_vma=False,
    )
```

time: 188 us -> 44 us (0.23)
  waiting for transfers between devices: 54.9 us -> 0 us
  local copies, waits for them, and re-layouts: 47.3 us -> 7 us
  matrix products: 40.1 us -> 0 us
  Pallas kernels: 0 us -> 35.5 us
  blocking collectives: 23.3 us -> 0 us
  between operations: 14.2 us -> 0.68 us
  other arithmetic: 5.11 us -> 0 us
  loops' own time: 2.73 us -> 0 us
    reduce_scatter x1 -> x0, waiting for transfers between devices: 54.9 us -> none  [per_device(): lax.psum_scatter(blocks.reshape(band_dev * lax.axis_size('row'), columns)...]
    dot_general x6 -> x0, matrix products: 40.1 us -> none  [the longest x4 29.8 us: apply_tile(): lax.dot_general(tile, density_block, (((1,), (1,)), ((), ())), preferred_...]
    pallas_call x0 -> x2, Pallas kernels: none -> 35.5 us  [the longest x1 25.3 us: per_device(): pl.pallas_call(functools.partial(pair_kernel, src_dev, row_total), out_sh...]
    gather x6 -> x0, local copies, waits for them, and re-layouts: 27.6 us -> none  [the longest x2 9.22 us: panel_geometry(): corner_three = vertices[:, corners[2]]]
    all_gather x1 -> x0, blocking collectives: 23.3 us -> none  [per_device(): lax.all_gather(own_centers[:, :band_dev], 'row', axis=1, tiled=True)]
    dynamic_update_slice x8 -> x0, local copies, waits for them, and re-layouts: 9.44 us -> none  [per_device(): lax.map(one_block, jnp.arange(band_dev * lax.axis_size('row') // block, d...]
    another operation x1 -> x0, local copies, waits for them, and re-layouts: 5.32 us -> none  [vertex_grid(): return jnp.stack([coord_x, coord_y, coord_z]).reshape(3, cycle_count * NPH)]
    unnamed x6 -> x17, local copies, waits for them, and re-layouts: 1.79 us -> 7 us
  transfers between devices with their start and end apart: 1 -> 0, of which waited for: 1 -> 0; matrix products, arithmetic and copies ran while one was open for 0% -> 0% of each run, Pallas kernels for 0% -> 0%
where the time goes in v1:
time: 44 us; the launch traced here: 43.2 us
  Pallas kernels  35.5 us (81%)
  local copies, waits for them, and re-layouts  7 us (16%)
  between operations  0.68 us (2%)
    pallas_call x1, Pallas kernels, per_device(): pl.pallas_call(functools.partial(pair_kernel, src_dev, row_total), out_sh...  25.3 us
    pallas_call x1, Pallas kernels, per_device(): pl.pallas_call(functools.partial(geometry_kernel, padded, src_dev, row_to...  10.2 us
    unnamed x17, local copies, waits for them, and re-layouts  7 us

profile of v1, /device:TPU:0, one launch (start us, length us, event | category | flops | bytes accessed | tf_op | source)
XLA Modules:
  0.0 43.2 jit_solution(2855592824309249764)
XLA Ops:
  0.7 0.0 copy-start
  0.7 1.0 %copy-done = s32[3,32768]{1,0:T(4,128)S(1)} copy-done((s32[3,32768]{1,0:T(4,128)S(1)}, s32[3,32768]{1,0:T(4,128)}, u32[]{:S(2)}) %copy-start) | copy-done | bytes 393240
  1.7 0.0 copy-start.2
  1.7 0.8 %copy-done.2 = f32[64,256]{1,0:T(8,128)S(1)} copy-done((f32[64,256]{1,0:T(8,128)S(1)}, f32[64,256]{1,0:T(8,128)}, u32[]{:S(2)}) %copy-start.2) | copy-done | bytes 65560
  2.5 0.0 copy-start.3
  2.5 0.8 %copy-done.3 = f32[80,64]{1,0:T(8,128)S(1)} copy-done((f32[80,64]{1,0:T(8,128)S(1)}, f32[80,64]{1,0:T(8,128)}, u32[]{:S(2)}) %copy-start.3) | copy-done | bytes 20504
  3.3 0.0 copy-start.4
  3.3 0.7 %copy-done.4 = s32[2,1024]{1,0:T(2,128)S(1)} copy-done((s32[2,1024]{1,0:T(2,128)S(1)}, s32[2,1024]{1,0:T(2,128)}, u32[]{:S(2)}) %copy-start.4) | copy-done | bytes 8216
  4.0 0.0 copy-start.5
  4.0 0.7 %copy-done.5 = bf16[16,256]{1,0:T(8,128)(2,1)S(1)} copy-done((bf16[16,256]{1,0:T(8,128)(2,1)S(1)}, bf16[16,256]{1,0:T(8,128)(2,1)}, u32[]{:S(2)}) %copy-start.5) | copy-done | bytes 8216
  4.7 0.0 copy-start.6
  4.7 0.7 %copy-done.6 = s32[1024]{0:T(1024)S(1)} copy-done((s32[1024]{0:T(1024)S(1)}, s32[1024]{0:T(1024)}, u32[]{:S(2)}) %copy-start.6) | copy-done | bytes 4120
  5.4 0.0 copy-start.7
  5.4 0.7 %copy-done.7 = bf16[16,80]{1,0:T(8,128)(2,1)S(1)} copy-done((bf16[16,80]{1,0:T(8,128)(2,1)S(1)}, bf16[16,80]{1,0:T(8,128)(2,1)}, u32[]{:S(2)}) %copy-start.7) | copy-done | bytes 2584
  6.1 10.2 %geometry.1 = (bf16[32,4096]{1,0:T(8,128)(2,1)S(1)}, f32[3,4096]{1,0:T(4,128)S(1)}, bf16[2048,32]{1,0:T(8,128)(2,1)S(1)}, f32[3,2048,128]{2,1,0:T(8,128)S(1)}) custom-call(s32[1]{0:T(128)S(6)} %copy.11.sample_ref, s32[1,1024]{1,0:T(1,128)S(1)} %bitcast.3, s32[2,1024]{1,0:T(2,128)S(1)} %copy-done.4, s32[3,32768]{1,0:T(4,128)S(1)} %copy-done, ...), custom_call_target="tpu_custom_call" | custom-call | tf_op jit(solution)/shard_map/geometry/pallas_call | solution.py:304
  16.3 0.0 copy-start.1
  16.3 0.9 %copy-done.1 = bf16[64,2048]{1,0:T(8,128)(2,1)S(1)} copy-done((bf16[64,2048]{1,0:T(8,128)(2,1)S(1)}, bf16[64,2048]{1,0:T(8,128)(2,1)}, u32[]{:S(2)}) %copy-start.1) | copy-done | bytes 262168
  17.3 25.3 %pairs.1 = f32[64,256]{1,0:T(8,128)S(1)} custom-call(bf16[32,4096]{1,0:T(8,128)(2,1)S(1)} %get-tuple-element.9.target_k_ref, f32[3,4096]{1,0:T(4,128)S(1)} %get-tuple-element.10.target_c_ref, bf16[2048,32]{1,0:T(8,128)(2,1)S(1)} %get-tuple-element.11.source_k_ref, f32[3,2048,128]{2,1,0:T(8,128)S(1)} %get-tuple-element.12.source_b_ref, ...), custom_call_target="tpu_custom_call" | custom-call | tf_op jit(solution)/shard_map/pairs/pallas_call | solution.py:324
  42.6 0.6 %copy.12 = f32[256,64]{0,1:T(8,128)} copy(f32[256,64]{0,1:T(8,128)S(1)} %bitcast.2) | data formatting | bytes 131072
Async XLA Ops:
  0.7 1.0 %copy-start = (s32[3,32768]{1,0:T(4,128)S(1)}, s32[3,32768]{1,0:T(4,128)}, u32[]{:S(2)}) copy-start(s32[3,32768]{1,0:T(4,128)} %conn_ref.1) | copy-start | bytes 1179652
  1.7 0.8 %copy-start.2 = (f32[64,256]{1,0:T(8,128)S(1)}, f32[64,256]{1,0:T(8,128)}, u32[]{:S(2)}) copy-start(f32[64,256]{1,0:T(8,128)} %constant.9.clone.azi_ref) | copy-start | bytes 196612
  2.5 0.8 %copy-start.3 = (f32[80,64]{1,0:T(8,128)S(1)}, f32[80,64]{1,0:T(8,128)}, u32[]{:S(2)}) copy-start(f32[80,64]{1,0:T(8,128)} %constant.8.clone.pol_ref) | copy-start | bytes 61444
  3.3 0.7 %copy-start.4 = (s32[2,1024]{1,0:T(2,128)S(1)}, s32[2,1024]{1,0:T(2,128)}, u32[]{:S(2)}) copy-start(s32[2,1024]{1,0:T(2,128)} %mode_ref.1) | copy-start | bytes 24580
  4.0 0.7 %copy-start.5 = (bf16[16,256]{1,0:T(8,128)(2,1)S(1)}, bf16[16,256]{1,0:T(8,128)(2,1)}, u32[]{:S(2)}) copy-start(bf16[16,256]{1,0:T(8,128)(2,1)} %constant.10.clone.azim_rows_ref) | copy-start | bytes 24580
  4.7 0.7 %copy-start.6 = (s32[1024]{0:T(1024)S(1)}, s32[1024]{0:T(1024)}, u32[]{:S(2)}) copy-start(s32[1024]{0:T(1024)} %param.10) | copy-start | bytes 12292
  5.4 0.7 %copy-start.7 = (bf16[16,80]{1,0:T(8,128)(2,1)S(1)}, bf16[16,80]{1,0:T(8,128)(2,1)}, u32[]{:S(2)}) copy-start(bf16[16,80]{1,0:T(8,128)(2,1)} %constant.11.clone.polar_rows_ref) | copy-start | bytes 7684
  16.3 1.0 %copy-start.1 = (bf16[64,2048]{1,0:T(8,128)(2,1)S(1)}, bf16[64,2048]{1,0:T(8,128)(2,1)}, u32[]{:S(2)}) copy-start(bf16[64,2048]{1,0:T(8,128)(2,1)} %density_ref.1) | copy-start | bytes 786436

commit v2 on v1

--- a/solution.py
+++ b/solution.py
@@ -17,7 +17,7 @@
 AZIM_LOW = -16
 KDIM = 32
 CHUNK = 256
-SRC_TILE = 256
+SRC_TILE = 512
 
 F32 = jnp.float32
 BF16 = jnp.bfloat16
@@ -80,8 +80,8 @@
     return jnp.dot(left, right, precision=lax.Precision.HIGHEST, preferred_element_type=F32)
 
 
-def geometry_kernel(
-    padded, src_dev, row_total,
+def geometry(
+    padded, src_dev, row_total, wait_conn,
     sample_ref, lattice_ref, mode_ref, conn_ref, pol_ref, azi_ref, azim_rows_ref, polar_rows_ref,
     target_k_ref, target_c_ref, source_k_ref, source_b_ref,
     table_ref, rows_ref,
@@ -108,6 +108,7 @@
         table_ref[index * padded:(index + 1) * padded, :] = part
     table_ref[6 * padded:6 * padded + 16, :] = azim_rows_ref[...]
     rows_ref[...] = jnp.zeros_like(rows_ref)
+    wait_conn()
 
     def corners_of(corner):
         azim_all = corner & (NPH - 1)
@@ -206,15 +207,29 @@
             )
         return carry
 
-    lax.fori_loop(0, row_total, target_chunk, 0)
-    lax.fori_loop(0, src_dev // CHUNK, source_chunk, 0)
-
-
-def pair_kernel(
-    src_dev, row_total,
-    target_k_ref, target_c_ref, source_k_ref, source_b_ref, density_ref,
-    out_ref, send_buf, recv_buf, send_sem, recv_sem,
+    lax.fori_loop(0, row_total, target_chunk, 0, unroll=4)
+    lax.fori_loop(0, src_dev // CHUNK, source_chunk, 0, unroll=4)
+
+
+def kernel(
+    padded, src_dev, row_total,
+    sample_ref, conn_hbm, density_hbm, lattice_hbm, mode_hbm, pol_hbm, azi_hbm, azim_rows_hbm,
+    polar_rows_hbm,
+    out_ref,
+    conn_ref, density_ref, lattice_ref, mode_ref, pol_ref, azi_ref, azim_rows_ref, polar_rows_ref,
+    target_k_ref, target_c_ref, source_k_ref, source_b_ref, table_ref, rows_ref,
+    send_buf, recv_buf, load_sem, send_sem, recv_sem,
 ):
+    loads = [
+        pltpu.make_async_copy(source, place, load_sem.at[index])
+        for index, (source, place) in enumerate((
+            (conn_hbm, conn_ref), (density_hbm, density_ref), (lattice_hbm, lattice_ref),
+            (mode_hbm, mode_ref), (pol_hbm, pol_ref), (azi_hbm, azi_ref),
+            (azim_rows_hbm, azim_rows_ref), (polar_rows_hbm, polar_rows_ref),
+        ))
+    ]
+    for index in (3, 2, 5, 4, 6, 7, 0, 1):
+        loads[index].start()
     me = lax.axis_index("row")
     peers = row_total - 1
 
@@ -228,15 +243,36 @@
         return carry
 
     lax.fori_loop(0, peers, greet, 0)
+    for load in loads[2:]:
+        load.wait()
+    geometry(
+        padded, src_dev, row_total, loads[0].wait,
+        sample_ref, lattice_ref, mode_ref, conn_ref, pol_ref, azi_ref, azim_rows_ref,
+        polar_rows_ref, target_k_ref, target_c_ref, source_k_ref, source_b_ref,
+        table_ref, rows_ref,
+    )
+    loads[1].wait()
 
     def block(owner, own):
         place = pl.ds(pl.multiple_of(owner * BAND_DEV, BAND_DEV), BAND_DEV)
         target_k = target_k_ref[:, place]
         target = [target_c_ref[axis:axis + 1, place] for axis in range(3)]
+        def numerator(first):
+            return jnp.dot(
+                source_k_ref[first:first + SRC_TILE, :], target_k, preferred_element_type=F32
+            )
+
+        def weigh(first, tile):
+            return jnp.dot(
+                density_ref[:, first:first + SRC_TILE], tile, preferred_element_type=F32
+            )
+
         total = jnp.zeros((density_ref.shape[0], BAND_DEV), F32)
+        top = numerator(0)
+        before = None
         for first in range(0, src_dev, SRC_TILE):
+            following = numerator(first + SRC_TILE) if first + SRC_TILE < src_dev else None
             part = slice(first, first + SRC_TILE)
-            top = jnp.dot(source_k_ref[part, :], target_k, preferred_element_type=F32)
             dist = None
             for axis in range(3):
                 wide = source_b_ref[axis, part, :]
@@ -252,8 +288,12 @@
             else:
                 inverse = lax.rsqrt(dist)
                 tile = top * inverse * (inverse * inverse)
-            total += jnp.dot(density_ref[:, part], tile.astype(BF16), preferred_element_type=F32)
-        return total
+            tile = tile.astype(BF16)
+            if before is not None:
+                total += weigh(first - SRC_TILE, before)
+            before = tile
+            top = following
+        return total + weigh(src_dev - SRC_TILE, before)
 
     def copy(turn):
         return pltpu.make_async_remote_copy(
@@ -301,42 +341,34 @@
     pol, azi, azim_rows, polar_rows = [jnp.asarray(t) for t in tables(cycle_count, padded)]
     vmem = pl.BlockSpec(memory_space=pltpu.VMEM)
     smem = pl.BlockSpec(memory_space=pltpu.SMEM)
-    target_k, target_c, source_k, source_b = pl.pallas_call(
-        functools.partial(geometry_kernel, padded, src_dev, row_total),
-        out_shape=[
-            jax.ShapeDtypeStruct((KDIM, band), BF16),
-            jax.ShapeDtypeStruct((3, band), F32),
-            jax.ShapeDtypeStruct((src_dev, KDIM), BF16),
-            jax.ShapeDtypeStruct((3, src_dev, 128), F32),
-        ],
-        in_specs=[smem] + [vmem] * 7,
-        out_specs=[vmem] * 4,
-        scratch_shapes=[
+    hbm = pl.BlockSpec(memory_space=pltpu.HBM)
+    loaded = [
+        connectivity, density, lattice_vector.reshape(1, -1), mode_table,
+        pol, azi, azim_rows, polar_rows,
+    ]
+    sums = pl.pallas_call(
+        functools.partial(kernel, padded, src_dev, row_total),
+        out_shape=jax.ShapeDtypeStruct((columns, BAND_DEV), F32),
+        in_specs=[smem] + [hbm] * len(loaded),
+        out_specs=vmem,
+        scratch_shapes=[pltpu.VMEM(array.shape, array.dtype) for array in loaded] + [
+            pltpu.VMEM((KDIM, band), BF16),
+            pltpu.VMEM((3, band), F32),
+            pltpu.VMEM((src_dev, KDIM), BF16),
+            pltpu.VMEM((3, src_dev, 128), F32),
             pltpu.VMEM((6 * padded + 16, NPH), BF16),
             pltpu.VMEM((KDIM + 8, CHUNK), F32),
-        ],
-        compiler_params=pltpu.CompilerParams(vmem_limit_bytes=40 << 20),
-        name="geometry",
-    )(
-        sample_index, lattice_vector.reshape(1, -1), mode_table, connectivity,
-        pol, azi, azim_rows, polar_rows,
-    )
-    sums = pl.pallas_call(
-        functools.partial(pair_kernel, src_dev, row_total),
-        out_shape=jax.ShapeDtypeStruct((columns, BAND_DEV), F32),
-        in_specs=[vmem] * 5,
-        out_specs=vmem,
-        scratch_shapes=[
             pltpu.VMEM((row_total - 1, columns, BAND_DEV), BF16),
             pltpu.VMEM((row_total - 1, columns, BAND_DEV), BF16),
+            pltpu.SemaphoreType.DMA((len(loaded),)),
             pltpu.SemaphoreType.DMA((row_total - 1,)),
             pltpu.SemaphoreType.DMA((row_total - 1,)),
         ],
         compiler_params=pltpu.CompilerParams(
             collective_id=0, has_side_effects=True, vmem_limit_bytes=40 << 20
         ),
-        name="pairs",
-    )(target_k, target_c, source_k, source_b, density)
+        name="potential",
+    )(sample_index, *loaded)
     return sums.T
 
 

time: 44 us -> 34.3 us (0.78)
  the two profiles are of different devices: /device:TPU:0 before, /device:TPU:1 now
where the time goes in v2:
time: 34.3 us; the launch traced here: 33.9 us
  Pallas kernels  26.9 us (78%)
  local copies, waits for them, and re-layouts  6.34 us (18%)
  between operations  0.68 us (2%)
    pallas_call x1, Pallas kernels, per_device(): pl.pallas_call(functools.partial(kernel, padded, src_dev, row_total), out...  26.9 us
    unnamed x17, local copies, waits for them, and re-layouts  6.34 us

profile of v2, /device:TPU:1, one launch (start us, length us, event | category | flops | bytes accessed | tf_op | source)
XLA Modules:
  0.0 33.9 jit_solution(11966932499725367342)
XLA Ops:
  0.0 0.0 copy-start.7
  0.7 0.0 copy-done.7
  0.7 0.0 copy-start
  0.7 1.0 %copy-done = s32[3,32768]{1,0:T(4,128)S(1)} copy-done((s32[3,32768]{1,0:T(4,128)S(1)}, s32[3,32768]{1,0:T(4,128)}, u32[]{:S(2)}) %copy-start) | copy-done | bytes 393240
  1.7 0.0 copy-start.1
  1.7 0.9 %copy-done.1 = bf16[64,2048]{1,0:T(8,128)(2,1)S(1)} copy-done((bf16[64,2048]{1,0:T(8,128)(2,1)S(1)}, bf16[64,2048]{1,0:T(8,128)(2,1)}, u32[]{:S(2)}) %copy-start.1) | copy-done | bytes 262168
  2.7 0.0 copy-start.2
  2.7 0.8 %copy-done.2 = f32[64,256]{1,0:T(8,128)S(1)} copy-done((f32[64,256]{1,0:T(8,128)S(1)}, f32[64,256]{1,0:T(8,128)}, u32[]{:S(2)}) %copy-start.2) | copy-done | bytes 65560
  3.5 0.0 copy-start.3
  3.5 0.8 %copy-done.3 = f32[80,64]{1,0:T(8,128)S(1)} copy-done((f32[80,64]{1,0:T(8,128)S(1)}, f32[80,64]{1,0:T(8,128)}, u32[]{:S(2)}) %copy-start.3) | copy-done | bytes 20504
  4.3 0.0 copy-start.4
  4.3 0.7 %copy-done.4 = s32[2,1024]{1,0:T(2,128)S(1)} copy-done((s32[2,1024]{1,0:T(2,128)S(1)}, s32[2,1024]{1,0:T(2,128)}, u32[]{:S(2)}) %copy-start.4) | copy-done | bytes 8216
  5.0 0.0 copy-start.5
  5.0 0.7 %copy-done.5 = bf16[16,256]{1,0:T(8,128)(2,1)S(1)} copy-done((bf16[16,256]{1,0:T(8,128)(2,1)S(1)}, bf16[16,256]{1,0:T(8,128)(2,1)}, u32[]{:S(2)}) %copy-start.5) | copy-done | bytes 8216
  5.7 0.0 copy-start.6
  5.7 0.7 %copy-done.6 = s32[1024]{0:T(1024)S(1)} copy-done((s32[1024]{0:T(1024)S(1)}, s32[1024]{0:T(1024)}, u32[]{:S(2)}) %copy-start.6) | copy-done | bytes 4120
  6.4 26.9 %potential.1 = f32[64,256]{1,0:T(8,128)S(1)} custom-call(s32[1]{0:T(128)S(6)} %copy.11.sample_ref, s32[3,32768]{1,0:T(4,128)S(1)} %copy-done, bf16[64,2048]{1,0:T(8,128)(2,1)S(1)} %copy-done.1, s32[1,1024]{1,0:T(1,128)S(1)} %bitcast.3, s32[2,1024]{1,0:T(2,128)S(1)} %copy-done.4, f32[80,64]{1,0:T(8,128)S(1)} %copy-done.3, f32[64,256]{1,0:T(8,128)S(1)} %copy-done.2, ...), custom_call_target="tpu_custom_call" | custom-call | tf_op jit(solution)/shard_map/potential/pallas_call | solution.py:349
  33.3 0.6 %copy.12 = f32[256,64]{0,1:T(8,128)} copy(f32[256,64]{0,1:T(8,128)S(1)} %bitcast.2) | data formatting | bytes 131072
Async XLA Ops:
  0.0 0.7 %copy-start.7 = (bf16[16,80]{1,0:T(8,128)(2,1)S(1)}, bf16[16,80]{1,0:T(8,128)(2,1)}, u32[]{:S(2)}) copy-start(bf16[16,80]{1,0:T(8,128)(2,1)} %constant.11.clone.polar_rows_hbm) | copy-start | bytes 7684
  0.7 1.0 %copy-start = (s32[3,32768]{1,0:T(4,128)S(1)}, s32[3,32768]{1,0:T(4,128)}, u32[]{:S(2)}) copy-start(s32[3,32768]{1,0:T(4,128)} %conn_hbm.1) | copy-start | bytes 1179652
  1.7 0.9 %copy-start.1 = (bf16[64,2048]{1,0:T(8,128)(2,1)S(1)}, bf16[64,2048]{1,0:T(8,128)(2,1)}, u32[]{:S(2)}) copy-start(bf16[64,2048]{1,0:T(8,128)(2,1)} %density_hbm.1) | copy-start | bytes 786436
  2.7 0.8 %copy-start.2 = (f32[64,256]{1,0:T(8,128)S(1)}, f32[64,256]{1,0:T(8,128)}, u32[]{:S(2)}) copy-start(f32[64,256]{1,0:T(8,128)} %constant.9.clone.azi_hbm) | copy-start | bytes 196612
  3.5 0.8 %copy-start.3 = (f32[80,64]{1,0:T(8,128)S(1)}, f32[80,64]{1,0:T(8,128)}, u32[]{:S(2)}) copy-start(f32[80,64]{1,0:T(8,128)} %constant.8.clone.pol_hbm) | copy-start | bytes 61444
  4.3 0.7 %copy-start.4 = (s32[2,1024]{1,0:T(2,128)S(1)}, s32[2,1024]{1,0:T(2,128)}, u32[]{:S(2)}) copy-start(s32[2,1024]{1,0:T(2,128)} %mode_hbm.1) | copy-start | bytes 24580
  5.0 0.7 %copy-start.5 = (bf16[16,256]{1,0:T(8,128)(2,1)S(1)}, bf16[16,256]{1,0:T(8,128)(2,1)}, u32[]{:S(2)}) copy-start(bf16[16,256]{1,0:T(8,128)(2,1)} %constant.10.clone.azim_rows_hbm) | copy-start | bytes 24580
  5.7 0.7 %copy-start.6 = (s32[1024]{0:T(1024)S(1)}, s32[1024]{0:T(1024)}, u32[]{:S(2)}) copy-start(s32[1024]{0:T(1024)} %param.10) | copy-start | bytes 12292

commit v3 on v2

--- a/solution.py
+++ b/solution.py
@@ -86,6 +86,8 @@
     target_k_ref, target_c_ref, source_k_ref, source_b_ref,
     table_ref, rows_ref,
 ):
+    me = lax.axis_index("row")
+    side_of_pair = lax.rem(me, 2)
     steps = (sample_ref[0] * lattice_ref[...]) & (NLAT - 1)
     shifts = steps.astype(F32) / NLAT - 0.5
     polar = mode_ref[0:1, :]
@@ -165,7 +167,7 @@
         return [(points[0][axis] + points[1][axis] + points[2][axis]) / 3.0 for axis in range(3)]
 
     def target_chunk(turn, carry):
-        first = pl.multiple_of(turn * src_dev, src_dev)
+        first = pl.multiple_of((2 * turn + side_of_pair) * src_dev, src_dev)
         center = center_of(corners_of(conn_ref[:, pl.ds(first, CHUNK)]))
         place = pl.ds(pl.multiple_of(turn * CHUNK, CHUNK), CHUNK)
         for axis in range(3):
@@ -178,7 +180,7 @@
         return carry
 
     def source_chunk(turn, carry):
-        first = pl.multiple_of(lax.axis_index("row") * src_dev + turn * CHUNK, CHUNK)
+        first = pl.multiple_of((me - side_of_pair) * src_dev + turn * CHUNK, CHUNK)
         points = corners_of(conn_ref[:, pl.ds(first, CHUNK)])
         center = center_of(points)
         one = [points[1][axis] - points[0][axis] for axis in range(3)]
@@ -207,8 +209,8 @@
             )
         return carry
 
-    lax.fori_loop(0, row_total, target_chunk, 0, unroll=4)
-    lax.fori_loop(0, src_dev // CHUNK, source_chunk, 0, unroll=4)
+    lax.fori_loop(0, 2 * src_dev // CHUNK, source_chunk, 0, unroll=8)
+    lax.fori_loop(0, row_total // 2, target_chunk, 0, unroll=8)
 
 
 def kernel(
@@ -218,43 +220,67 @@
     out_ref,
     conn_ref, density_ref, lattice_ref, mode_ref, pol_ref, azi_ref, azim_rows_ref, polar_rows_ref,
     target_k_ref, target_c_ref, source_k_ref, source_b_ref, table_ref, rows_ref,
-    send_buf, recv_buf, load_sem, send_sem, recv_sem,
+    send_buf, recv_buf, load_sem, share_sem, send_sem, recv_sem,
 ):
+    me = lax.axis_index("row")
+    side = lax.rem(me, 2)
+    sibling = me + 1 - 2 * side
+    owners = row_total // 2
+    own_half = pl.ds(pl.multiple_of(side * src_dev, src_dev), src_dev)
     loads = [
         pltpu.make_async_copy(source, place, load_sem.at[index])
         for index, (source, place) in enumerate((
-            (conn_hbm, conn_ref), (density_hbm, density_ref), (lattice_hbm, lattice_ref),
+            (conn_hbm, conn_ref), (density_hbm, density_ref.at[:, own_half]), (lattice_hbm, lattice_ref),
             (mode_hbm, mode_ref), (pol_hbm, pol_ref), (azi_hbm, azi_ref),
             (azim_rows_hbm, azim_rows_ref), (polar_rows_hbm, polar_rows_ref),
         ))
     ]
     for index in (3, 2, 5, 4, 6, 7, 0, 1):
         loads[index].start()
-    me = lax.axis_index("row")
-    peers = row_total - 1
+    peers = owners - 1
+
+    def owner_of(turn):
+        return 2 * lax.rem(me // 2 + 1 + turn, owners) + side
 
     barrier = pltpu.get_barrier_semaphore()
+    pl.semaphore_signal(
+        barrier, inc=1, device_id={"row": sibling}, device_id_type=pl.DeviceIdType.MESH
+    )
 
     def greet(turn, carry):
-        other = lax.rem(me + 1 + turn, row_total)
         pl.semaphore_signal(
-            barrier, inc=1, device_id={"row": other}, device_id_type=pl.DeviceIdType.MESH
+            barrier, inc=1, device_id={"row": owner_of(turn)}, device_id_type=pl.DeviceIdType.MESH
         )
         return carry
 
     lax.fori_loop(0, peers, greet, 0)
+    share = pltpu.make_async_remote_copy(
+        src_ref=density_ref.at[:, own_half],
+        dst_ref=density_ref.at[:, own_half],
+        send_sem=share_sem.at[0],
+        recv_sem=share_sem.at[1],
+        device_id={"row": sibling},
+        device_id_type=pl.DeviceIdType.MESH,
+    )
+
+    def begin():
+        loads[0].wait()
+        loads[1].wait()
+        pl.semaphore_wait(barrier, peers + 1)
+        share.start()
+
     for load in loads[2:]:
         load.wait()
     geometry(
-        padded, src_dev, row_total, loads[0].wait,
+        padded, src_dev, row_total, begin,
         sample_ref, lattice_ref, mode_ref, conn_ref, pol_ref, azi_ref, azim_rows_ref,
         polar_rows_ref, target_k_ref, target_c_ref, source_k_ref, source_b_ref,
         table_ref, rows_ref,
     )
-    loads[1].wait()
-
-    def block(owner, own):
-        place = pl.ds(pl.multiple_of(owner * BAND_DEV, BAND_DEV), BAND_DEV)
+    share.wait()
+
+    def block(place_index, own):
+        place = pl.ds(pl.multiple_of(place_index * BAND_DEV, BAND_DEV), BAND_DEV)
         target_k = target_k_ref[:, place]
         target = [target_c_ref[axis:axis + 1, place] for axis in range(3)]
         def numerator(first):
@@ -270,18 +296,18 @@
         total = jnp.zeros((density_ref.shape[0], BAND_DEV), F32)
         top = numerator(0)
         before = None
-        for first in range(0, src_dev, SRC_TILE):
-            following = numerator(first + SRC_TILE) if first + SRC_TILE < src_dev else None
+        for first in range(0, 2 * src_dev, SRC_TILE):
+            following = numerator(first + SRC_TILE) if first + SRC_TILE < 2 * src_dev else None
             part = slice(first, first + SRC_TILE)
             dist = None
             for axis in range(3):
                 wide = source_b_ref[axis, part, :]
                 diff = target[axis] - jnp.concatenate([wide] * (BAND_DEV // 128), axis=1)
                 dist = diff * diff if dist is None else dist + diff * diff
-            if own and first < BAND_DEV:
+            if own and first % src_dev < BAND_DEV:
                 same = (
                     lax.broadcasted_iota(jnp.int32, dist.shape, 0) + first
-                    == lax.broadcasted_iota(jnp.int32, dist.shape, 1)
+                    == lax.broadcasted_iota(jnp.int32, dist.shape, 1) + side * src_dev
                 )
                 inverse = lax.rsqrt(jnp.where(same, 1.0, dist))
                 tile = jnp.where(same, 0.0, top * inverse * (inverse * inverse))
@@ -293,7 +319,7 @@
                 total += weigh(first - SRC_TILE, before)
             before = tile
             top = following
-        return total + weigh(src_dev - SRC_TILE, before)
+        return total + weigh(2 * src_dev - SRC_TILE, before)
 
     def copy(turn):
         return pltpu.make_async_remote_copy(
@@ -301,21 +327,18 @@
             dst_ref=recv_buf.at[turn],
             send_sem=send_sem.at[turn],
             recv_sem=recv_sem.at[turn],
-            device_id={"row": lax.rem(me + 1 + turn, row_total)},
+            device_id={"row": owner_of(turn)},
             device_id_type=pl.DeviceIdType.MESH,
         )
 
-    send_buf[0] = block(lax.rem(me + 1, row_total), False).astype(BF16)
-    pl.semaphore_wait(barrier, peers)
-    copy(0).start()
-
     def step(turn, carry):
-        send_buf[turn] = block(lax.rem(me + 1 + turn, row_total), False).astype(BF16)
+        send_buf[turn] = block(lax.rem(me // 2 + 1 + turn, owners), False).astype(BF16)
         copy(turn).start()
         return carry
 
-    lax.fori_loop(1, peers, step, 0)
-    out_ref[...] = block(me, True) + 0.5 * density_ref[:, 0:BAND_DEV].astype(F32)
+    lax.fori_loop(0, peers, step, 0)
+    local = density_ref[:, pl.ds(pl.multiple_of(side * src_dev, src_dev), BAND_DEV)]
+    out_ref[...] = block(me // 2, True) + 0.5 * local.astype(F32)
 
     def collect(turn, carry):
         copy(turn).wait_recv()
@@ -351,21 +374,25 @@
         out_shape=jax.ShapeDtypeStruct((columns, BAND_DEV), F32),
         in_specs=[smem] + [hbm] * len(loaded),
         out_specs=vmem,
-        scratch_shapes=[pltpu.VMEM(array.shape, array.dtype) for array in loaded] + [
-            pltpu.VMEM((KDIM, band), BF16),
-            pltpu.VMEM((3, band), F32),
-            pltpu.VMEM((src_dev, KDIM), BF16),
-            pltpu.VMEM((3, src_dev, 128), F32),
+        scratch_shapes=[
+            pltpu.VMEM(connectivity.shape, jnp.int32),
+            pltpu.VMEM((columns, 2 * src_dev), BF16),
+        ] + [pltpu.VMEM(array.shape, array.dtype) for array in loaded[2:]] + [
+            pltpu.VMEM((KDIM, band // 2), BF16),
+            pltpu.VMEM((3, band // 2), F32),
+            pltpu.VMEM((2 * src_dev, KDIM), BF16),
+            pltpu.VMEM((3, 2 * src_dev, 128), F32),
             pltpu.VMEM((6 * padded + 16, NPH), BF16),
             pltpu.VMEM((KDIM + 8, CHUNK), F32),
-            pltpu.VMEM((row_total - 1, columns, BAND_DEV), BF16),
-            pltpu.VMEM((row_total - 1, columns, BAND_DEV), BF16),
+            pltpu.VMEM((row_total // 2 - 1, columns, BAND_DEV), BF16),
+            pltpu.VMEM((row_total // 2 - 1, columns, BAND_DEV), BF16),
             pltpu.SemaphoreType.DMA((len(loaded),)),
-            pltpu.SemaphoreType.DMA((row_total - 1,)),
-            pltpu.SemaphoreType.DMA((row_total - 1,)),
+            pltpu.SemaphoreType.DMA((2,)),
+            pltpu.SemaphoreType.DMA((row_total // 2 - 1,)),
+            pltpu.SemaphoreType.DMA((row_total // 2 - 1,)),
         ],
         compiler_params=pltpu.CompilerParams(
-            collective_id=0, has_side_effects=True, vmem_limit_bytes=40 << 20
+            collective_id=0, has_side_effects=True, vmem_limit_bytes=63 << 20
         ),
         name="potential",
     )(sample_index, *loaded)

time: 34.3 us -> 30.8 us (0.90)
  the two profiles are of different devices: /device:TPU:1 before, /device:TPU:0 now
where the time goes in v3:
time: 30.8 us; the launch traced here: 30.6 us
  Pallas kernels  28.4 us (92%)
  local copies, waits for them, and re-layouts  1.47 us (5%)
  between operations  0.66 us (2%)
    pallas_call x1, Pallas kernels, per_device(): pl.pallas_call(functools.partial(kernel, padded, src_dev, row_total), out...  28.4 us
    unnamed x1, local copies, waits for them, and re-layouts  1.47 us

profile of v3, /device:TPU:0, one launch (start us, length us, event | category | flops | bytes accessed | tf_op | source)
XLA Modules:
  0.0 30.6 jit_solution(7386110242674579997)
XLA Ops:
  0.7 28.4 %potential.1 = f32[64,256]{1,0:T(8,128)} custom-call(s32[1]{0:T(128)S(6)} %copy.11.sample_ref, s32[3,32768]{1,0:T(4,128)} %conn_hbm.1, bf16[64,2048]{1,0:T(8,128)(2,1)} %density_hbm.1, s32[1,1024]{1,0:T(1,128)} %bitcast.3, s32[2,1024]{1,0:T(2,128)} %mode_hbm.1, f32[80,64]{1,0:T(8,128)} %constant.8.clone.pol_hbm, f32[64,256]{1,0:T(8,128)} %constant.9.clone.azi_hbm, ...), custom_call_target="tpu_custom_call" | custom-call | tf_op jit(solution)/shard_map/potential/pallas_call | solution.py:372
  29.1 1.5 %copy.12 = f32[256,64]{0,1:T(8,128)} copy(f32[256,64]{0,1:T(8,128)} %bitcast.2) | data formatting | bytes 131072
